TPU v7x, 256 devices: a whole 4x4x8 slice. The times are simulated.
256 devices in a mesh: cell: 32 (over z_hi, x, core), mode: 8 (over z_lo, y).
Axes of the slice: x: 4, y: 4, z: 8 (z_hi: 4, z_lo: 2; z = z_hi * 2 + z_lo), core: 2. Of those that a mesh axis runs over, the one named last changes fastest.
Arguments:
- pod_modes: bfloat16 [3, 512, 4, 64, 128], P(None, 'mode', None, 'cell'), may hold values from -6 to 6
- slab_map: int32 [4, 64, 128], P(None, 'cell'), may hold values from 0 to 7
- slab_volume: float32 [8], replicated, may hold values from 0.25 to 4
- advect_index: int32 [8], replicated, may hold values from 0 to 511, as said below
- pair_adv: int32 [2048], replicated, may hold values from 0 to 7
- pair_mode: int32 [2048], replicated, may hold values from 0 to 511
- pair_amp: float32 [2048, 1024], replicated, may hold values from -0.2 to 0.2
Outputs:
- convective: float32 [512, 8, 512], P(('mode', 'cell'))
- response: float32 [512, 1024], P(('mode', 'cell'))
Inputs may be any that keep to these rules, and one draw needn't show every extreme that they name: `advect_index`: 8 distinct mode indices.
All inputs are finite; a program needn't handle non-finite values.
Results may differ from a plain program's by a relative error of at most 0.0043.
Values may be sent and summed in bfloat16 or wider, within the bound.
A program may use at most 128 MiB of HBM per device.

v0:
```python
import jax
import jax.numpy as jnp
from jax import lax
from jax.sharding import PartitionSpec as P


def split_up(x, dim, size):
    lengths = x.shape
    blocks = x.reshape(*lengths[:dim], size, lengths[dim] // size, *lengths[dim + 1 :])
    return jnp.moveaxis(blocks, dim, 0)


def sum_at_owner(x, axis, dim):
    blocks = split_up(x, dim, lax.axis_size(axis))
    arrived = lax.all_to_all(blocks, axis, split_axis=0, concat_axis=0, tiled=True)
    return arrived.sum(axis=0)


def padded(x, sides, width):
    for axis, dim in sides:
        size, length = (lax.axis_size(axis), x.shape[dim])
        up = [(i, (i + 1) % size) for i in range(size - 1)]
        down = [(j, i) for i, j in up]
        last = lax.slice_in_dim(x, length - width, length, axis=dim)
        first = lax.slice_in_dim(x, 0, width, axis=dim)
        before = lax.ppermute(last, axis, up)
        after = lax.ppermute(first, axis, down)
        x = jnp.concatenate([before, x, after], axis=dim)
    return x


def from_everyone(x, axis):
    copies = jnp.broadcast_to(x, (lax.axis_size(axis), *x.shape))
    return lax.all_to_all(copies, axis, split_axis=0, concat_axis=0, tiled=True)


def of_everyone(x, axis):
    everything = from_everyone(x, axis)
    return jnp.sum(everything.astype(jnp.float32), axis=0)


def gradients(haloed):
    interior = haloed[:, :, :, 1:-1].astype(jnp.float32)
    along_x = 0.5 * (jnp.roll(interior, -1, axis=2) - jnp.roll(interior, 1, axis=2))
    along_y = 0.5 * (
        haloed[:, :, :, 2:].astype(jnp.float32) - haloed[:, :, :, :-2].astype(jnp.float32)
    )
    along_z = 0.5 * (jnp.roll(interior, -1, axis=4) - jnp.roll(interior, 1, axis=4))
    return jnp.stack([along_x, along_y, along_z]).astype(jnp.bfloat16)


def contract(left_factor, grads):
    return jnp.einsum("ijdcxyz,dckxyz->ijk", left_factor, grads, preferred_element_type=jnp.float32)


def owner_rows(partial_value):
    return sum_at_owner(partial_value, "cell", 0)


def shards(pod_modes, slab_map, slab_volume, advect_index, pair_adv, pair_mode, pair_amp):
    mode_block = pod_modes.shape[1]
    planes = pod_modes.shape[2]
    rows_y = pod_modes.shape[3]
    cols_z = pod_modes.shape[4]
    mode_devs = lax.axis_size("mode")
    cell_devs = lax.axis_size("cell")
    mode_count = mode_block * mode_devs
    advect_count = advect_index.shape[0]
    scale_factor = float(planes * rows_y * cell_devs * cols_z) ** (-0.5)
    haloed = padded(pod_modes, (("cell", 3),), 1)
    first_mode = lax.axis_index("mode") * mode_block
    slots = lax.broadcasted_iota(jnp.int32, (advect_count, mode_block), 1)
    owned = (advect_index[:, None] == first_mode + slots).astype(jnp.bfloat16)
    picked = jnp.einsum("jm,cmxyz->cjxyz", owned, pod_modes, preferred_element_type=jnp.float32)
    chosen = of_everyone(picked.astype(jnp.bfloat16), "mode").astype(jnp.float32)
    levels = slab_volume.shape[0]
    level_ids = lax.broadcasted_iota(jnp.int32, (levels, planes, rows_y, cols_z), 0)
    volume = jnp.sum(
        jnp.where(slab_map[None] == level_ids, slab_volume[:, None, None, None], 0.0), axis=0
    )
    weighted = chosen * volume[None, None]
    left_factor = (
        jnp.transpose(pod_modes, (1, 0, 2, 3, 4))[:, None, None, :].astype(jnp.float32)
        * jnp.transpose(weighted, (1, 0, 2, 3, 4))[None, :, :, None]
    ).astype(jnp.bfloat16)
    local_grads = gradients(haloed)
    block_part = contract(left_factor, lax.all_gather(local_grads, "mode", axis=2, tiled=True))
    owned_rows = owner_rows(block_part)
    tensor = owned_rows * scale_factor
    flat_rows = tensor.reshape(tensor.shape[0], advect_count * mode_count)
    pair_slot = pair_adv * mode_count + pair_mode
    columns = jnp.take(flat_rows, pair_slot, axis=1)
    response = jnp.dot(
        columns, pair_amp, precision=lax.Precision.HIGHEST, preferred_element_type=jnp.float32
    )
    return (tensor, response)


def solution(mesh):
    in_specs = (P(None, "mode", None, "cell", None), P(None, "cell", None), P(), P(), P(), P(), P())
    out_specs = (P(("mode", "cell"), None, None), P(("mode", "cell"), None))
    return jax.shard_map(shards, mesh=mesh, in_specs=in_specs, out_specs=out_specs, check_vma=False)
```

profile of v0, /device:TPU:32, one launch (start us, length us, event | category | flops | bytes accessed | tf_op | source)
XLA Modules:
  0.0 200.7 jit_solution(4320587217358106295)
XLA Ops:
  7.2 0.0 all-gather.2.cloned.1.call-start
  7.2 1.2 convert_bitcast_fusion
  8.4 0.8 fusion.23
  9.2 1.3 collective-permute-start
  10.5 3.7 %collective-permute-start.1 = (bf16[3,64,4,1,128]{4,1,3,2,0:T(8,128)(2,1)}, bf16[3,64,4,1,128]{4,1,3,2,0:T(8,128)(2,1)}, u32[]{:S(2)}, u32[]{:S(2)}) collective-permute-start(bf16[3,64,4,1,128]{4,1,3,2,0:T(8,128)(2,1)} %get-tuple-element.14), channel_id=1, source_target_pairs={{0,8},{8,16},{16,24},{24,32},{32,40},{40,48},{48,56},{56,64},{64,7... | collective-permute-start | bytes 589832 | tf_op jit(solution)/shard_map/ppermute | solution.py:26
  14.2 0.3 fusion.22
  14.5 1.2 slice_bitcast_fusion
  15.7 1.2 slice_bitcast_fusion.2
  16.9 0.8 slice_bitcast_fusion.4
  17.7 0.0 copy-start.3
  17.7 0.3 copy.49
  18.0 0.3 copy.50
  18.3 0.3 copy.51
  18.6 0.3 copy.52
  19.0 0.0 copy-start.4
  19.0 0.0 copy-start.5
  19.0 2.2 %fusion.9 = (bf16[1,3,64,4,2,128]{5,2,4,3,0,1:T(8,128)(2,1)S(1)}, bf16[1,3,64,4,2,128]{5,2,4,3,0,1:T(8,128)(2,1)S(1)}) fusion(f32[1,3,64,1,2,128]{5,2,4,3,1,0:T(8,128)} %get-tuple-element.3, f32[1,3,64,3,2,128]{5,2,4,3,1,0:T(8,128)} %get-tuple-element.5, f32[1,3,64,3,2,128]{5,2,4,3,0,1:T(8,128)} %get-tuple-element.4, ...), kind=kLoop, calls=%fused_computation.16 | loop fusion | flops 1966080 | bytes 3932160 | tf_op jit(solution)/shard_map/convert.1
  21.2 0.0 collective-permute-done
  21.2 0.0 collective-permute-done.1
  21.3 1.2 fusion.15
  22.4 1.2 pad_maximum_fusion
  23.6 0.0 all-gather.2.cloned.1.call-update
  23.6 0.0 copy-done.4
  23.6 1.2 fusion.4
  24.9 0.8 broadcast_in_dim.33
  25.7 5.9 %all-to-all-start = ((bf16[8,3,8,4,2,128]{5,2,4,3,1,0:T(8,128)(2,1)}), bf16[8,3,8,4,2,128]{5,2,4,3,1,0:T(8,128)(2,1)S(1)}, u32[]{:S(2)}, u32[]{:S(2)}) async-start(bf16[8,3,8,4,2,128]{5,2,4,3,1,0:T(8,128)(2,1)} %broadcast_in_dim.33), calls=%async_computation | async-start | bytes 786432 | tf_op jit(solution)/shard_map/all_to_all | solution.py:34
  31.6 0.6 copy.40
  32.2 0.0 copy-done.3
  32.3 0.0 copy-done.5
  32.3 0.1 select_reduce_fusion
  32.4 7.1 %all-to-all-done = bf16[8,3,8,4,2,128]{5,2,4,3,1,0:T(8,128)(2,1)S(1)} async-done(((bf16[8,3,8,4,2,128]{5,2,4,3,1,0:T(8,128)(2,1)}), bf16[8,3,8,4,2,128]{5,2,4,3,1,0:T(8,128)(2,1)S(1)}, u32[]{:S(2)}, u32[]{:S(2)}) %all-to-all-start) | async-done | bytes 393248 | tf_op jit(solution)/shard_map/all_to_all | solution.py:34
  39.5 0.1 convert_reduce_fusion
  39.5 0.0 copy-start.1
  39.6 0.0 copy-start.2
  39.6 92.9 %all-gather.2.cloned.1.call-done = bf16[3,3,512,4,2,128]{5,2,4,3,0,1:T(8,128)(2,1)} async-done(((bf16[3,3,64,4,2,128]{5,2,4,3,0,1:T(8,128)(2,1)}), bf16[3,3,512,4,2,128]{5,2,4,3,0,1:T(8,128)(2,1)}) %all-gather.2.cloned.1.call-update) | async-done | bytes 9437200 | tf_op jit(solution)/shard_map/all_gather | solution.py:87
  132.4 8.4 %fusion = f32[64,8,512,1,1,1,1]{2,1,6,0,5,4,3:T(8,128)} fusion(bf16[3,3,512,4,2,128]{5,2,4,3,0,1:T(8,128)(2,1)} %all-gather.2.cloned.1.call-done, f32[8,3,4,2,128]{4,0,3,2,1:T(8,128)S(1)} %multiply_bitcast_fusion, f32[64,3,4,2,128]{4,3,0,2,1:T(2,128)S(1)} %copy.40), kind=kOutput, calls=%fused_computation.2 | convolution fusion | flops 4841275392 | bytes 11370496 | tf_op jit(solution)/shard_map/ijdcxyz,dckxyz->ijk/dot_general | solution.py:53
  140.8 9.8 %all-to-all-start.1 = ((f32[32,2,8,512]{3,2,1,0:T(8,128)}), f32[32,2,8,512]{3,2,1,0:T(8,128)S(1)}, u32[]{:S(2)}, u32[]{:S(2)}) async-start(f32[32,2,8,512]{3,2,1,0:T(8,128)} %bitcast.22), calls=%async_computation.1 | async-start | bytes 2097152 | tf_op jit(solution)/shard_map/all_to_all | solution.py:15
  150.7 0.0 copy-done.1
  150.7 0.0 copy-done.2
  150.7 29.8 %all-to-all-done.1 = f32[32,2,8,512]{3,2,1,0:T(8,128)S(1)} async-done(((f32[32,2,8,512]{3,2,1,0:T(8,128)}), f32[32,2,8,512]{3,2,1,0:T(8,128)S(1)}, u32[]{:S(2)}, u32[]{:S(2)}) %all-to-all-start.1) | async-done | bytes 1048608 | tf_op jit(solution)/shard_map/all_to_all | solution.py:15
  180.5 0.1 reduce_sum.29
  180.6 0.0 copy-start
  180.6 0.6 copy.54
  181.3 5.5 %gather_fusion = f32[2048,2]{1,0:T(8,128)S(1)} fusion(f32[2,4096]{0,1:T(8,128)S(1)} %bitcast.57, s32[2048]{0:T(1024)S(1)} %broadcast_clamp_fusion), kind=kCustom, calls=%fused_computation | custom fusion | bytes 40960 | tf_op jit(solution)/shard_map/jit(_take)/gather | solution.py:92
  186.7 7.1 %fusion.5 = f32[2,1024]{1,0:T(2,128)} fusion(f32[2048,1024]{1,0:T(8,128)} %param.13, f32[2048,2]{1,0:T(8,128)S(1)} %gather_fusion, pred[2048]{0:T(1024)(128)(4,1)S(1)} %compare_and_fusion), kind=kOutput, calls=%fused_computation.9 | convolution fusion | flops 50335744 | bytes 8415232 | tf_op jit(solution)/shard_map/dot_general | solution.py:93
  193.9 0.0 copy-done
  (5 shorter events, 0.0 us)
Async XLA Ops:
  7.2 125.3 %all-gather.2.cloned.1.call-start = ((), (), s32[]{:S(2)}) async-start(), calls=%async_computation.2 | async-start | bytes 10616832 | tf_op jit(solution)/shard_map/all_gather | solution.py:87
  9.2 12.0 %collective-permute-start = (bf16[3,64,4,1,128]{4,1,3,2,0:T(8,128)(2,1)}, bf16[3,64,4,1,128]{4,1,3,2,0:T(8,128)(2,1)}, u32[]{:S(2)}, u32[]{:S(2)}) collective-permute-start(bf16[3,64,4,1,128]{4,1,3,2,0:T(8,128)(2,1)} %get-tuple-element.13), channel_id=1, source_target_pairs={{8,0},{16,8},{24,16},{32,24},{40,32},{48,40},{56,48},{64,56},{72,6... | collective-permute-start | bytes 589832 | tf_op jit(solution)/shard_map/ppermute | solution.py:27
  10.5 10.7 %collective-permute-start.1 = (bf16[3,64,4,1,128]{4,1,3,2,0:T(8,128)(2,1)}, bf16[3,64,4,1,128]{4,1,3,2,0:T(8,128)(2,1)}, u32[]{:S(2)}, u32[]{:S(2)}) collective-permute-start(bf16[3,64,4,1,128]{4,1,3,2,0:T(8,128)(2,1)} %get-tuple-element.14), channel_id=1, source_target_pairs={{0,8},{8,16},{16,24},{24,32},{32,40},{40,48},{48,56},{56,64},{64,7... | collective-permute-start | bytes 589832 | tf_op jit(solution)/shard_map/ppermute | solution.py:26
  17.7 14.6 %copy-start.3 = (s32[4,2,128]{2,1,0:T(2,128)S(1)}, s32[4,2,128]{2,1,0:T(2,128)}, u32[]{:S(2)}) copy-start(s32[4,2,128]{2,1,0:T(2,128)} %param.8) | copy-start | bytes 12292
  19.0 4.7 %copy-start.4 = (s32[8]{0:T(128)S(1)}, s32[8]{0:T(128)}, u32[]{:S(2)}) copy-start(s32[8]{0:T(128)} %param.10) | copy-start | bytes 100
  19.0 13.3 %copy-start.5 = (f32[8]{0:T(128)S(1)}, f32[8]{0:T(128)}, u32[]{:S(2)}) copy-start(f32[8]{0:T(128)} %param.9) | copy-start | bytes 100
  25.7 13.8 %all-to-all-start = ((bf16[8,3,8,4,2,128]{5,2,4,3,1,0:T(8,128)(2,1)}), bf16[8,3,8,4,2,128]{5,2,4,3,1,0:T(8,128)(2,1)S(1)}, u32[]{:S(2)}, u32[]{:S(2)}) async-start(bf16[8,3,8,4,2,128]{5,2,4,3,1,0:T(8,128)(2,1)} %broadcast_in_dim.33), calls=%async_computation | async-start | bytes 786432 | tf_op jit(solution)/shard_map/all_to_all | solution.py:34
  39.5 111.1 %copy-start.1 = (s32[2048]{0:T(1024)S(1)}, s32[2048]{0:T(1024)}, u32[]{:S(2)}) copy-start(s32[2048]{0:T(1024)} %param.12) | copy-start | bytes 24580
  39.6 111.1 %copy-start.2 = (s32[2048]{0:T(1024)S(1)}, s32[2048]{0:T(1024)}, u32[]{:S(2)}) copy-start(s32[2048]{0:T(1024)} %param.11) | copy-start | bytes 24580
  140.8 39.7 %all-to-all-start.1 = ((f32[32,2,8,512]{3,2,1,0:T(8,128)}), f32[32,2,8,512]{3,2,1,0:T(8,128)S(1)}, u32[]{:S(2)}, u32[]{:S(2)}) async-start(f32[32,2,8,512]{3,2,1,0:T(8,128)} %bitcast.22), calls=%async_computation.1 | async-start | bytes 2097152 | tf_op jit(solution)/shard_map/all_to_all | solution.py:15
  180.6 13.3 %copy-start = (f32[2,8,512]{2,1,0:T(8,128)}, f32[2,8,512]{2,1,0:T(8,128)S(1)}, u32[]{:S(2)}) copy-start(f32[2,8,512]{2,1,0:T(8,128)S(1)} %broadcast_multiply_fusion) | copy-start | bytes 98308
Sparse Core Ops, SparseCore 0:
  23.7 108.6 all-gather.1
where the time goes:
time: 201 us
  waiting for transfers between devices  130 us (65%)
  starting transfers between devices  20.8 us (10%)
  matrix products  16.8 us (8%)
  between operations  14.2 us (7%)
  local copies, waits for them, and re-layouts  13.1 us (7%)
  other arithmetic  6.06 us (3%)
    all_gather x1, waiting for transfers between devices, shards(): lax.all_gather(local_grads, 'mode', axis=2, tiled=True)  92.9 us
    all_to_all x1, waiting for transfers between devices, sum_at_owner(): lax.all_to_all(blocks, axis, split_axis=0, concat_axis=0, tiled=True)  29.8 us
    all_to_all x1, starting transfers between devices, sum_at_owner(): lax.all_to_all(blocks, axis, split_axis=0, concat_axis=0, tiled=True)  9.82 us
    dot_general x1, matrix products, contract(): jnp.einsum('ijdcxyz,dckxyz->ijk', left_factor, grads, preferred_element_t...  8.4 us
    dot_general x1, matrix products, shards(): jnp.dot(columns, pair_amp, precision=lax.Precision.HIGHEST, preferred_ele...  7.14 us
    all_to_all x1, waiting for transfers between devices, from_everyone(): return lax.all_to_all(copies, axis, split_axis=0, concat_axis=0, tiled=True)  7.12 us
    all_to_all x1, starting transfers between devices, from_everyone(): return lax.all_to_all(copies, axis, split_axis=0, concat_axis=0, tiled=True)  5.93 us
    gather x1, local copies, waits for them, and re-layouts, shards(): columns = jnp.take(flat_rows, pair_slot, axis=1)  5.47 us
  transfers between devices with their start and end apart: 5, of which 3 were waited for; matrix products, arithmetic and copies ran while one was open for 5% of the time, Pallas kernels for 0%

commit v1 on v0

--- a/solution.py
+++ b/solution.py
@@ -84,7 +84,12 @@
         * jnp.transpose(weighted, (1, 0, 2, 3, 4))[None, :, :, None]
     ).astype(jnp.bfloat16)
     local_grads = gradients(haloed)
-    block_part = contract(left_factor, lax.all_gather(local_grads, "mode", axis=2, tiled=True))
+    block_part = contract(
+        left_factor,
+        jnp.concatenate(
+            lax.all_to_all(jnp.stack([local_grads] * lax.axis_size("mode")), "mode", 0, 0), axis=2
+        ),
+    )
     owned_rows = owner_rows(block_part)
     tensor = owned_rows * scale_factor
     flat_rows = tensor.reshape(tensor.shape[0], advect_count * mode_count)

time: 201 us -> 225 us (1.12)
  local copies, waits for them, and re-layouts: 13.1 us -> 35.2 us
  between operations: 14.2 us -> 0.83 us
  starting transfers between devices: 20.8 us -> 27.2 us
  other arithmetic: 6.06 us -> 11.1 us
  waiting for transfers between devices: 130 us -> 133 us
    all_to_all x0 -> x1, waiting for transfers between devices: none -> 103 us  [shards(): lax.all_to_all(jnp.stack([local_grads] * lax.axis_size('mode')), 'mode',...]
    all_gather x1 -> x0, waiting for transfers between devices: 92.9 us -> none  [shards(): lax.all_gather(local_grads, 'mode', axis=2, tiled=True)]
    reshape x0 -> x1, local copies, waits for them, and re-layouts: none -> 10.7 us  [shards(): jnp.concatenate(lax.all_to_all(jnp.stack([local_grads] * lax.axis_size('m...]
    all_to_all x1, waiting for transfers between devices: 7.12 us -> 0.01 us  [from_everyone(): return lax.all_to_all(copies, axis, split_axis=0, concat_axis=0, tiled=True)]
    another operation x0 -> x2, local copies, waits for them, and re-layouts: none -> 6.41 us  [the longest x1 6.11 us: shards(): jnp.stack([local_grads] * lax.axis_size('mode'))]
    all_to_all x0 -> x1, starting transfers between devices: none -> 5.84 us  [shards(): lax.all_to_all(jnp.stack([local_grads] * lax.axis_size('mode')), 'mode',...]
    another operation x2, other arithmetic: 2.33 us -> 4.96 us  [gradients(): return jnp.stack([along_x, along_y, along_z]).astype(jnp.bfloat16)]
  transfers between devices with their start and end apart: 5 -> 5, of which waited for: 3 -> 2; matrix products, arithmetic and copies ran while one was open for 5% -> 10% of each run, Pallas kernels for 0% -> 0%
where the time goes in v1:
time: 225 us; the launch traced here: 224 us
  waiting for transfers between devices  133 us (59%)
  local copies, waits for them, and re-layouts  35.2 us (16%)
  starting transfers between devices  27.2 us (12%)
  matrix products  16.8 us (7%)
  other arithmetic  11.1 us (5%)
    all_to_all x1, waiting for transfers between devices, shards(): lax.all_to_all(jnp.stack([local_grads] * lax.axis_size('mode')), 'mode',...  103 us
    all_to_all x1, waiting for transfers between devices, sum_at_owner(): lax.all_to_all(blocks, axis, split_axis=0, concat_axis=0, tiled=True)  29.8 us
    reshape x1, local copies, waits for them, and re-layouts, shards(): jnp.concatenate(lax.all_to_all(jnp.stack([local_grads] * lax.axis_size('m...  10.7 us
    all_to_all x1, starting transfers between devices, sum_at_owner(): lax.all_to_all(blocks, axis, split_axis=0, concat_axis=0, tiled=True)  10.4 us
    dot_general x1, matrix products, contract(): jnp.einsum('ijdcxyz,dckxyz->ijk', left_factor, grads, preferred_element_t...  8.44 us
    dot_general x1, matrix products, shards(): jnp.dot(columns, pair_amp, precision=lax.Precision.HIGHEST, preferred_ele...  7.14 us
    another operation x1, local copies, waits for them, and re-layouts, shards(): jnp.stack([local_grads] * lax.axis_size('mode'))  6.11 us
    all_to_all x1, starting transfers between devices, from_everyone(): return lax.all_to_all(copies, axis, split_axis=0, concat_axis=0, tiled=True)  5.93 us
  transfers between devices with their start and end apart: 5, of which 2 were waited for; matrix products, arithmetic and copies ran while one was open for 10% of the time, Pallas kernels for 0%

profile of v1, /device:TPU:32, one launch (start us, length us, event | category | flops | bytes accessed | tf_op | source)
XLA Modules:
  0.0 224.1 jit_solution(17770327876457495778)
XLA Ops:
  0.6 0.0 copy-start
  0.6 2.8 %fusion.20 = (bf16[3,64,4,1,128]{4,3,2,1,0:T(2,128)(2,1)}, bf16[3,64,4,1,128]{4,3,2,1,0:T(2,128)(2,1)}) fusion(bf16[3,64,4,2,128]{4,3,2,1,0:T(2,128)(2,1)} %param.7), kind=kLoop, calls=%fused_computation.44 | loop fusion | bytes 786432 | tf_op jit(solution)/shard_map/slice | solution.py:25
  3.4 1.3 collective-permute-start
  4.7 3.8 %collective-permute-start.1 = (bf16[3,64,4,1,128]{4,3,2,1,0:T(2,128)(2,1)}, bf16[3,64,4,1,128]{4,3,2,1,0:T(2,128)(2,1)}, u32[]{:S(2)}, u32[]{:S(2)}) collective-permute-start(bf16[3,64,4,1,128]{4,3,2,1,0:T(2,128)(2,1)} %get-tuple-element.9), channel_id=1, source_target_pairs={{0,8},{8,16},{16,24},{24,32},{32,40},{40,48},{48,56},{56,64},{64,7... | collective-permute-start | bytes 589832 | tf_op jit(solution)/shard_map/ppermute | solution.py:26
  8.5 1.2 fusion.4
  9.7 0.8 broadcast_in_dim.33
  10.6 5.9 %all-to-all-start = ((bf16[8,3,8,4,2,128]{5,2,4,3,1,0:T(8,128)(2,1)}), bf16[8,3,8,4,2,128]{5,2,4,3,1,0:T(8,128)(2,1)}, u32[]{:S(2)}, u32[]{:S(2)}) async-start(bf16[8,3,8,4,2,128]{5,2,4,3,1,0:T(8,128)(2,1)} %broadcast_in_dim.33), calls=%async_computation | async-start | bytes 786432 | tf_op jit(solution)/shard_map/all_to_all | solution.py:34
  16.5 1.3 mul.91
  17.8 2.0 slice_bitcast_fusion
  19.7 1.5 slice_bitcast_fusion.2
  21.2 0.9 slice_bitcast_fusion.4
  22.1 0.0 copy-done
  22.1 0.7 fusion.21
  22.8 0.8 copy.41
  23.6 0.9 copy.42
  24.5 0.8 copy.43
  25.3 0.9 copy.44
  26.2 3.6 %fusion.8 = (bf16[1,3,64,4,2,128]{5,4,3,2,1,0:T(2,128)(2,1)S(1)}, bf16[1,3,64,4,2,128]{5,4,3,2,1,0:T(2,128)(2,1)S(1)}) fusion(f32[1,3,64,1,2,128]{5,4,3,2,1,0:T(2,128)} %get-tuple-element.3, f32[1,3,64,3,2,128]{5,4,3,2,1,0:T(2,128)} %get-tuple-element.5, f32[1,3,64,3,2,128]{5,4,3,2,1,0:T(2,128)} %get-tuple-element.4, ...), kind=kLoop, calls=%fused_computation.15 | loop fusion | flops 1966080 | bytes 3932160 | tf_op jit(solution)/shard_map/convert.2
  29.8 0.0 collective-permute-done
  29.8 0.0 collective-permute-done.1
  29.8 2.9 %fusion.13 = bf16[1,3,64,4,2,128]{5,4,3,2,1,0:T(2,128)(2,1)S(1)} fusion(bf16[3,64,4,2,128]{4,3,2,1,0:T(2,128)(2,1)S(1)} %copy-done, bf16[3,64,4,1,128]{4,3,2,1,0:T(2,128)(2,1)} %collective-permute-done.1, bf16[3,64,4,1,128]{4,3,2,1,0:T(2,128)(2,1)} %collective-permute-done), kind=kLoop, calls=%fused_computation.25 | loop fusion | flops 2162688 | bytes 1179648 | tf_op jit(solution)/shard_map/stack | solution.py:49
  32.8 2.0 pad_maximum_fusion
  34.8 0.3 copy.45
  35.1 0.0 all-to-all-done
  35.1 6.1 %stack.8 = bf16[8,3,3,64,4,2,128]{6,3,5,4,1,2,0:T(8,128)(2,1)} broadcast(bf16[3,3,64,4,2,128]{5,2,4,3,0,1:T(8,128)(2,1)S(1)} %copy.45), dimensions={1,2,3,4,5,6} | broadcast | bytes 10616832 | tf_op jit(solution)/shard_map/stack | solution.py:90
  41.2 0.0 copy-start.4
  41.3 0.0 copy-start.5
  41.3 5.8 %all-to-all-start.1 = ((bf16[8,3,3,64,4,2,128]{6,3,5,4,1,2,0:T(8,128)(2,1)}), bf16[8,3,3,64,4,2,128]{6,3,5,4,1,2,0:T(8,128)(2,1)}, u32[]{:S(2)}, u32[]{:S(2)}) async-start(bf16[8,3,3,64,4,2,128]{6,3,5,4,1,2,0:T(8,128)(2,1)} %stack.8), calls=%async_computation.1 | async-start | bytes 18874368 | tf_op jit(solution)/shard_map/all_to_all | solution.py:90
  47.1 0.0 copy-done.4
  47.1 0.0 copy-done.5
  47.1 0.1 select_reduce_fusion
  47.2 1.1 convert_reduce_fusion
  48.3 103.1 %all-to-all-done.1 = bf16[8,3,3,64,4,2,128]{6,3,5,4,1,2,0:T(8,128)(2,1)} async-done(((bf16[8,3,3,64,4,2,128]{6,3,5,4,1,2,0:T(8,128)(2,1)}), bf16[8,3,3,64,4,2,128]{6,3,5,4,1,2,0:T(8,128)(2,1)}, u32[]{:S(2)}, u32[]{:S(2)}) %all-to-all-start.1) | async-done | bytes 9437216 | tf_op jit(solution)/shard_map/all_to_all | solution.py:90
  151.4 10.7 %copy.46 = bf16[3,3,8,64,4,2,128]{6,3,2,5,4,0,1:T(8,128)(2,1)} copy(bf16[3,3,8,64,4,2,128]{6,3,5,4,0,1,2:T(8,128)(2,1)} %bitcast.17) | data formatting | bytes 18874368 | tf_op jit(solution)/shard_map/reshape | solution.py:89
  162.1 0.0 copy-start.2
  162.1 0.0 copy-start.3
  162.1 8.4 %fusion.3 = f32[32,2,8,512]{3,2,1,0:T(8,128)} fusion(bf16[3,3,512,4,2,128,1,1]{5,2,4,3,7,6,0,1:T(8,128)(2,1)} %bitcast.46, f32[8,3,4,2,128]{4,0,3,2,1:T(8,128)S(1)} %multiply_bitcast_fusion, f32[32,2,3,4,2,128]{5,4,3,1,0,2:T(2,128)S(1)} %bitcast.45), kind=kOutput, calls=%fused_computation.5 | convolution fusion | flops 4841275392 | bytes 11370496 | tf_op jit(solution)/shard_map/ijdcxyz,dckxyz->ijk/dot_general | solution.py:53
  170.5 10.4 %all-to-all-start.2 = ((f32[32,2,8,512]{3,2,1,0:T(8,128)}), f32[32,2,8,512]{3,2,1,0:T(8,128)S(1)}, u32[]{:S(2)}, u32[]{:S(2)}) async-start(f32[32,2,8,512]{3,2,1,0:T(8,128)} %fusion.3), calls=%async_computation.2 | async-start | bytes 2097152 | tf_op jit(solution)/shard_map/all_to_all | solution.py:15
  180.9 0.0 copy-done.2
  180.9 0.0 copy-done.3
  181.0 29.8 %all-to-all-done.2 = f32[32,2,8,512]{3,2,1,0:T(8,128)S(1)} async-done(((f32[32,2,8,512]{3,2,1,0:T(8,128)}), f32[32,2,8,512]{3,2,1,0:T(8,128)S(1)}, u32[]{:S(2)}, u32[]{:S(2)}) %all-to-all-start.2) | async-done | bytes 1048608 | tf_op jit(solution)/shard_map/all_to_all | solution.py:15
  210.7 0.1 reduce_sum.29
  210.8 0.0 copy-start.1
  210.8 0.6 copy.47
  211.5 5.5 %gather_fusion = f32[2048,2]{1,0:T(8,128)S(1)} fusion(f32[2,4096]{0,1:T(8,128)S(1)} %bitcast.47, s32[2048]{0:T(1024)S(1)} %broadcast_clamp_fusion), kind=kCustom, calls=%fused_computation | custom fusion | bytes 40960 | tf_op jit(solution)/shard_map/jit(_take)/gather | solution.py:97
  216.9 7.1 %fusion.5 = f32[2,1024]{1,0:T(2,128)} fusion(f32[2048,1024]{1,0:T(8,128)} %param.13, f32[2048,2]{1,0:T(8,128)S(1)} %gather_fusion, pred[2048]{0:T(1024)(128)(4,1)S(1)} %compare_and_fusion), kind=kOutput, calls=%fused_computation.9 | convolution fusion | flops 50335744 | bytes 8415232 | tf_op jit(solution)/shard_map/dot_general | solution.py:98
  224.1 0.0 copy-done.1
  (5 shorter events, 0.0 us)
Async XLA Ops:
  0.6 21.4 %copy-start = (bf16[3,64,4,2,128]{4,3,2,1,0:T(2,128)(2,1)S(1)}, bf16[3,64,4,2,128]{4,3,2,1,0:T(2,128)(2,1)}, u32[]{:S(2)}) copy-start(bf16[3,64,4,2,128]{4,3,2,1,0:T(2,128)(2,1)} %param.7) | copy-start | bytes 1179652
  3.4 26.4 %collective-permute-start = (bf16[3,64,4,1,128]{4,3,2,1,0:T(2,128)(2,1)}, bf16[3,64,4,1,128]{4,3,2,1,0:T(2,128)(2,1)}, u32[]{:S(2)}, u32[]{:S(2)}) collective-permute-start(bf16[3,64,4,1,128]{4,3,2,1,0:T(2,128)(2,1)} %get-tuple-element.8), channel_id=1, source_target_pairs={{8,0},{16,8},{24,16},{32,24},{40,32},{48,40},{56,48},{64,56},{72,6... | collective-permute-start | bytes 589832 | tf_op jit(solution)/shard_map/ppermute | solution.py:27
  4.7 25.2 %collective-permute-start.1 = (bf16[3,64,4,1,128]{4,3,2,1,0:T(2,128)(2,1)}, bf16[3,64,4,1,128]{4,3,2,1,0:T(2,128)(2,1)}, u32[]{:S(2)}, u32[]{:S(2)}) collective-permute-start(bf16[3,64,4,1,128]{4,3,2,1,0:T(2,128)(2,1)} %get-tuple-element.9), channel_id=1, source_target_pairs={{0,8},{8,16},{16,24},{24,32},{32,40},{40,48},{48,56},{56,64},{64,7... | collective-permute-start | bytes 589832 | tf_op jit(solution)/shard_map/ppermute | solution.py:26
  10.6 24.6 %all-to-all-start = ((bf16[8,3,8,4,2,128]{5,2,4,3,1,0:T(8,128)(2,1)}), bf16[8,3,8,4,2,128]{5,2,4,3,1,0:T(8,128)(2,1)}, u32[]{:S(2)}, u32[]{:S(2)}) async-start(bf16[8,3,8,4,2,128]{5,2,4,3,1,0:T(8,128)(2,1)} %broadcast_in_dim.33), calls=%async_computation | async-start | bytes 786432 | tf_op jit(solution)/shard_map/all_to_all | solution.py:34
  41.2 5.8 %copy-start.4 = (s32[4,2,128]{2,1,0:T(2,128)S(1)}, s32[4,2,128]{2,1,0:T(2,128)}, u32[]{:S(2)}) copy-start(s32[4,2,128]{2,1,0:T(2,128)} %param.8) | copy-start | bytes 12292
  41.3 5.8 %copy-start.5 = (f32[8]{0:T(128)S(1)}, f32[8]{0:T(128)}, u32[]{:S(2)}) copy-start(f32[8]{0:T(128)} %param.9) | copy-start | bytes 100
  41.3 110.1 %all-to-all-start.1 = ((bf16[8,3,3,64,4,2,128]{6,3,5,4,1,2,0:T(8,128)(2,1)}), bf16[8,3,3,64,4,2,128]{6,3,5,4,1,2,0:T(8,128)(2,1)}, u32[]{:S(2)}, u32[]{:S(2)}) async-start(bf16[8,3,3,64,4,2,128]{6,3,5,4,1,2,0:T(8,128)(2,1)} %stack.8), calls=%async_computation.1 | async-start | bytes 18874368 | tf_op jit(solution)/shard_map/all_to_all | solution.py:90
  162.1 18.8 %copy-start.2 = (s32[2048]{0:T(1024)S(1)}, s32[2048]{0:T(1024)}, u32[]{:S(2)}) copy-start(s32[2048]{0:T(1024)} %param.12) | copy-start | bytes 24580
  162.1 18.8 %copy-start.3 = (s32[2048]{0:T(1024)S(1)}, s32[2048]{0:T(1024)}, u32[]{:S(2)}) copy-start(s32[2048]{0:T(1024)} %param.11) | copy-start | bytes 24580
  170.5 40.2 %all-to-all-start.2 = ((f32[32,2,8,512]{3,2,1,0:T(8,128)}), f32[32,2,8,512]{3,2,1,0:T(8,128)S(1)}, u32[]{:S(2)}, u32[]{:S(2)}) async-start(f32[32,2,8,512]{3,2,1,0:T(8,128)} %fusion.3), calls=%async_computation.2 | async-start | bytes 2097152 | tf_op jit(solution)/shard_map/all_to_all | solution.py:15
  210.8 13.3 %copy-start.1 = (f32[2,8,512]{2,1,0:T(8,128)}, f32[2,8,512]{2,1,0:T(8,128)S(1)}, u32[]{:S(2)}) copy-start(f32[2,8,512]{2,1,0:T(8,128)S(1)} %broadcast_multiply_fusion) | copy-start | bytes 98308
